TPU v7x, 32 devices: a whole 2x2x4 slice. The times are simulated.
32 devices in a mesh: space: 16 (over z, x, core), trial: 2 (over y).
Axes of the slice: x: 2, y: 2, z: 4, core: 2. Of those that a mesh axis runs over, the one named last changes fastest.
Arguments:
- trial_x: bfloat16 [4, 4096, 1024], P('trial', 'space')
- h_panel: bfloat16 [4096, 640], P('space')
- s_panel: bfloat16 [4096, 640], P('space')
- pattern: int32 [64, 10], P('space'), may hold values from 0 to 63, as said below
Outputs:
- theta: float32 [4], P('trial')
- new_dirs: bfloat16 [4, 4096, 1024], P('trial', 'space')
- mean_sq: float32 [4], P('trial')
Inputs may be any that keep to these rules, and one draw needn't show every extreme that they name: pattern[a, 0] is a; the entries of a row are distinct atoms of a's own spatial domain or of the two domains beside it (cyclically), the domain of atom a being a // 4.
All inputs are finite; a program needn't handle non-finite values.
Results may differ from a plain program's by a relative error of at most 0.0006.
Values may be sent and summed in bfloat16 or wider, within the bound.
A program may use at most 128 MiB of HBM per device.

v0:
```python
import jax
import jax.numpy as jnp
from jax import lax
from jax.sharding import PartitionSpec as P


def padded(x, sides, width):
    for axis, dim in sides:
        peers, length = (lax.axis_size(axis), x.shape[dim])
        up = [(i, (i + 1) % peers) for i in range(peers)]
        down = [(j, i) for i, j in up]
        last = lax.slice_in_dim(x, length - width, length, axis=dim)
        first = lax.slice_in_dim(x, 0, width, axis=dim)
        before = lax.ppermute(last, axis, up)
        after = lax.ppermute(first, axis, down)
        x = jnp.concatenate([before, x, after], axis=dim)
    return x


def neighbours(values, width):
    return padded(values, (("space", 1),), width)


def apply_tiles(h_panel, s_panel, links, extended, block):
    count, ext_rows, width = extended.shape
    atom_dev, slots = links.shape
    blocks = extended.reshape(count, ext_rows // block, block, width)
    picked = blocks[:, links]
    h_tiles = h_panel.reshape(atom_dev, block, slots, block)
    s_tiles = s_panel.reshape(atom_dev, block, slots, block)
    h_image = jnp.einsum("apbq,kabqw->kapw", h_tiles, picked, preferred_element_type=jnp.float32)
    s_image = jnp.einsum("apbq,kabqw->kapw", s_tiles, picked, preferred_element_type=jnp.float32)
    return (h_image.reshape(count, -1), s_image.reshape(count, -1))


def row_reduce(section, values):
    if section == "ritz":
        return lax.psum(values, "space")
    if section == "project":
        return lax.psum(values, "space")
    return lax.psum(values, "space")


def solve_coeffs(gram, correlation):
    factor = jnp.linalg.cholesky(gram)
    return jax.scipy.linalg.cho_solve((factor, True), correlation)


def finish(x_every, mine_shape, flat_h, flat_s, reducer, total):
    flat_all = x_every.reshape(x_every.shape[0], -1)
    gram_part = jnp.dot(flat_all, flat_all.T, preferred_element_type=jnp.float32)
    wide_all = flat_all.astype(jnp.float32)
    cross = jnp.sum(flat_s * flat_h, axis=1)
    weight = jnp.sum(flat_s * flat_s, axis=1)
    cross, weight, gram = reducer("ritz", (cross, weight, gram_part))
    theta = cross / (weight + 1e-06)
    flat_r = flat_h - theta[:, None] * flat_s
    correlation = reducer("project", jnp.dot(wide_all, flat_r.T, precision=lax.Precision.HIGHEST))
    coeffs = solve_coeffs(gram, correlation)
    normal_part = flat_r - jnp.dot(coeffs.T, wide_all, precision=lax.Precision.HIGHEST)
    mean_sq = reducer("norm", jnp.sum(normal_part * normal_part, axis=1)) / total
    scaled = normal_part * lax.rsqrt(mean_sq + 1e-06)[:, None]
    return (theta, scaled.astype(jnp.bfloat16).reshape(mine_shape), mean_sq)


def on_device(trial_x, h_panel, s_panel, pattern):
    atom_dev = pattern.shape[0]
    block = h_panel.shape[0] // atom_dev
    domains = lax.axis_size("space")
    atoms = atom_dev * domains
    links = jnp.mod(pattern - lax.axis_index("space") * atom_dev + atom_dev, atoms)
    total = float(atoms * block * trial_x.shape[2])
    x_every = lax.all_gather(trial_x, "trial", axis=0, tiled=True)
    flat_h, flat_s = apply_tiles(
        h_panel, s_panel, links, neighbours(trial_x, atom_dev * block), block
    )
    theta, normed, mean_sq = finish(x_every, trial_x.shape, flat_h, flat_s, row_reduce, total)
    return (theta, normed, mean_sq)


def solution(mesh):
    in_specs = (P("trial", "space", None), P("space", None), P("space", None), P("space", None))
    out_specs = (P("trial"), P("trial", "space", None), P("trial"))
    return jax.shard_map(
        on_device, mesh=mesh, in_specs=in_specs, out_specs=out_specs, check_vma=False
    )
```

profile of v0, /device:TPU:0, one launch (start us, length us, event | category | flops | bytes accessed | tf_op | source)
XLA Modules:
  0.0 193.6 jit_solution(5035406191406211222)
XLA Ops:
  7.2 0.0 copy-start.8
  7.2 0.0 all-gather.2.cloned.1.call-start
  7.2 0.5 collective-permute-start
  7.7 5.0 %collective-permute-start.1 = (bf16[2,256,1024]{2,1,0:T(8,128)(2,1)}, bf16[2,256,1024]{2,1,0:T(8,128)(2,1)}, u32[]{:S(2)}, u32[]{:S(2)}) collective-permute-start(bf16[2,256,1024]{2,1,0:T(8,128)(2,1)} %param.4), channel_id=1, source_target_pairs={{2,0},{4,2},{6,4},{8,6},{10,8},{12,10},{14,12},{16,14},{18,16},{20... | collective-permute-start | bytes 3145736 | tf_op jit(solution)/shard_map/ppermute | solution.py:15
  12.8 0.0 all-gather.2.cloned.1.call-update
  12.8 0.7 compare_select_fusion
  13.5 0.1 reshape.56
  13.6 2.4 %reshape.70 = bf16[4,64,10,64]{3,2,1,0:T(8,128)(2,1)} reshape(bf16[256,640]{1,0:T(8,128)(2,1)} %param.5) | data formatting | bytes 655360 | tf_op jit(solution)/shard_map/reshape | solution.py:29
  16.0 0.0 copy-done.8
  16.0 1.6 reshape.69
  17.6 7.9 %collective-permute-done = bf16[2,256,1024]{2,1,0:T(8,128)(2,1)S(1)} collective-permute-done((bf16[2,256,1024]{2,1,0:T(8,128)(2,1)}, bf16[2,256,1024]{2,1,0:T(8,128)(2,1)S(1)}, u32[]{:S(2)}, u32[]{:S(2)}) %collective-permute-start) | collective-permute-done | bytes 1048608 | tf_op jit(solution)/shard_map/ppermute | solution.py:14
  25.5 0.0 copy-start.7
  25.5 1.0 copy-done.7
  26.5 0.0 collective-permute-done.1
  26.5 2.0 %pad_maximum_fusion = bf16[2,768,1024]{2,1,0:T(8,128)(2,1)S(1)} fusion(bf16[2,256,1024]{2,1,0:T(8,128)(2,1)} %collective-permute-done.1, bf16[2,256,1024]{2,1,0:T(8,128)(2,1)} %param.4, bf16[2,256,1024]{2,1,0:T(8,128)(2,1)} %copy-done.7), kind=kLoop, calls=%fused_computation.6 | loop fusion | flops 9437184 | bytes 6291456 | tf_op jit(solution)/shard_map/concatenate | solution.py:16
  28.5 5.8 %gather_fusion = bf16[40,2,64,1024]{3,2,1,0:T(8,128)(2,1)} fusion(bf16[2,12,64,1024]{3,2,1,0:T(8,128)(2,1)S(1)} %bitcast.54, s32[1024]{0:T(1024)S(1)} %pad_clamp_fusion), kind=kCustom, calls=%fused_computation | custom fusion | bytes 20971680 | tf_op jit(solution)/shard_map/gather | solution.py:28
  34.2 0.0 copy-start
  34.2 0.0 copy-start.6
  34.2 6.5 %fusion.6 = f32[2,4,64,1024]{3,2,0,1:T(8,128)S(1)} fusion(bf16[2,4,10,64,1024]{4,3,0,2,1:T(8,128)(2,1)} %bitcast.55, bf16[4,64,10,64,1]{3,2,1,0,4:T(8,128)(2,1)} %bitcast.68), kind=kOutput, calls=%fused_computation.14 | convolution fusion | flops 671088640 | bytes 12910592 | tf_op jit(solution)/shard_map/apbq,kabqw->kapw/dot_general | solution.py:31
  40.7 0.8 copy-done
  41.5 0.2 copy-done.6
  41.7 3.5 %multiply_reduce_fusion.1 = (f32[2]{0:T(128)S(1)}, f32[2]{0:T(128)S(1)}, f32[2,4,64,1024]{3,2,0,1:T(8,128)}) fusion(f32[2,4,64,1024]{3,2,0,1:T(8,128)S(1)} %fusion.6, bf16[2,4,10,64,1024]{4,3,0,2,1:T(8,128)(2,1)S(1)} %bitcast.56, bf16[4,64,10,64,1]{3,2,1,0,4:T(8,128)(2,1)S(1)} %bitcast.67), kind=kOutput, calls=%fused_computation.10 | convolution fusion | flops 673185792 | bytes 15007760 | tf_op jit(solution)/shard_map/apbq,kabqw->kapw/dot_general | solution.py:32
  45.2 39.5 %all-reduce.1 = (f32[2]{0:T(128)S(1)}, f32[2]{0:T(128)S(1)}) all-reduce(f32[2]{0:T(128)S(1)} %get-tuple-element.4, f32[2]{0:T(128)S(1)} %get-tuple-element.3), channel_id=1, replica_groups=mesh['space'=16,'trial'=2] {'space'}, use_global_device_ids=true, to_apply=%region_1.2 | all-reduce | flops 4 | bytes 32 | tf_op jit(solution)/shard_map/psum | solution.py:38
  84.8 0.0 copy-start.1
  84.8 1.4 copy.32
  86.2 0.9 copy-done.1
  87.1 0.1 copy.33
  87.3 0.0 copy-start.9
  87.3 0.5 multiply_subtract_fusion
  87.8 0.1 copy.39
  87.9 2.9 %copy.56 = f32[1,2,256,1024]{3,1,2,0:T(2,128)} copy(f32[1,2,256,1024]{3,2,1,0:T(8,128)S(1)} %bitcast.59) | data formatting | bytes 4194304
  90.9 1.6 copy.55
  92.5 0.0 all-gather.2.cloned.1.call-done
  92.5 0.0 copy-start.5
  92.5 3.4 %copy.57 = bf16[1,4,256,1024]{3,1,2,0:T(4,128)(2,1)S(1)} copy(bf16[1,4,256,1024]{3,2,1,0:T(8,128)(2,1)} %bitcast.61) | data formatting | bytes 4194304
  95.9 0.0 copy-start.4
  95.9 1.3 copy-done.4
  97.2 0.0 copy-done.5
  97.2 0.0 copy-start.3
  97.2 9.2 %convolution_bitcast_fusion = f32[4,2]{0,1:T(2,128)S(1)} fusion(f32[2,262144]{1,0:T(2,128)S(1)} %bitcast.66, bf16[4,262144]{1,0:T(4,128)(2,1)S(1)} %bitcast.63), kind=kOutput, calls=%fused_computation.17 | convolution fusion | flops 25165824 | bytes 4194336 | tf_op jit(solution)/shard_map/dot_general | solution.py:58
  106.4 0.0 copy-done.3
  106.4 0.0 copy-start.2
  106.4 3.5 %fusion.12 = f32[4,4]{0,1:T(4,128)S(1)} fusion(bf16[4,256,1024]{2,1,0:T(8,128)(2,1)S(1)} %copy-done.3), kind=kOutput, calls=%fused_computation.16 | convolution fusion | flops 8388608 | bytes 2097216 | tf_op jit(solution)/shard_map/dot_general | solution.py:51
  109.9 0.0 copy-done.2
  109.9 2.9 %copy.54 = f32[1,2,256,1024]{3,1,2,0:T(2,128)} copy(f32[1,2,256,1024]{3,2,1,0:T(8,128)S(1)} %bitcast.57) | data formatting | bytes 4194304
  112.9 29.5 %all-reduce = (f32[4,2]{0,1:T(2,128)S(1)}, f32[4,4]{0,1:T(4,128)S(1)}) all-reduce(f32[4,2]{0,1:T(2,128)S(1)} %convolution_bitcast_fusion, f32[4,4]{0,1:T(4,128)S(1)} %fusion.12), channel_id=1, replica_groups=mesh['space'=16,'trial'=2] {'space'}, use_global_device_ids=true, to_apply=%region_7.8 | all-reduce | flops 24 | bytes 192 | tf_op jit(solution)/shard_map/psum | solution.py:40
  142.3 0.1 copy.37
  142.4 0.4 cholesky.16
  142.8 0.6 compare_reduce_fusion
  143.5 0.6 fusion.17
  144.1 0.3 custom-call.10
  144.5 0.1 fusion.19
  144.6 0.1 fusion.21
  144.7 0.0 copy-done.9
  144.7 8.7 %multiply_reduce_fusion = (f32[2]{0:T(128)S(1)}, f32[2,262144]{1,0:T(2,128)}) fusion(f32[4,2]{0,1:T(2,128)S(1)} %fusion.21, bf16[4,262144]{1,0:T(4,128)(2,1)} %bitcast.64, f32[2,262144]{1,0:T(2,128)} %bitcast.65, f32[2,262144]{1,0:T(2,128)S(1)} %bitcast.62, f32[2]{0:T(128)S(1)} %add_divide_fusion), kind=kOutput, calls=%fused_computation.8 | convolution fusion | flops 27787262 | bytes 8388656 | tf_op jit(solution)/shard_map/dot_general | solution.py:60
  153.4 29.5 %psum.39 = f32[2]{0:T(128)S(1)} all-reduce(f32[2]{0:T(128)S(1)} %get-tuple-element.12), channel_id=1, replica_groups=mesh['space'=16,'trial'=2] {'space'}, use_global_device_ids=true, to_apply=%region_9.10 | all-reduce | flops 2 | bytes 16 | tf_op jit(solution)/shard_map/psum | solution.py:41
  182.9 0.5 add_rsqrt_fusion
  183.4 2.1 %multiply_convert_fusion = bf16[2,262144]{1,0:T(2,128)(2,1)S(1)} fusion(f32[2,262144]{1,0:T(2,128)} %get-tuple-element.13, f32[2]{0:T(128)S(1)} %get-tuple-element.9), kind=kLoop, calls=%fused_computation.7 | loop fusion | flops 1048576 | bytes 3145736 | tf_op jit(solution)/shard_map/convert_element_type | solution.py:63
  185.6 1.2 copy.80
  (4 shorter events, 0.0 us)
Async XLA Ops:
  7.2 8.8 %copy-start.8 = (bf16[256,640]{1,0:T(8,128)(2,1)S(1)}, bf16[256,640]{1,0:T(8,128)(2,1)}, u32[]{:S(2)}) copy-start(bf16[256,640]{1,0:T(8,128)(2,1)} %param.6) | copy-start | bytes 983044
  7.2 85.3 %all-gather.2.cloned.1.call-start = ((), (), s32[]{:S(2)}) async-start(), calls=%async_computation | async-start | bytes 3145728 | tf_op jit(solution)/shard_map/all_gather | solution.py:73
  7.2 18.3 %collective-permute-start = (bf16[2,256,1024]{2,1,0:T(8,128)(2,1)}, bf16[2,256,1024]{2,1,0:T(8,128)(2,1)S(1)}, u32[]{:S(2)}, u32[]{:S(2)}) collective-permute-start(bf16[2,256,1024]{2,1,0:T(8,128)(2,1)} %param.4), channel_id=1, source_target_pairs={{0,2},{2,4},{4,6},{6,8},{8,10},{10,12},{12,14},{14,16},{16,18},{18... | collective-permute-start | bytes 3145736 | tf_op jit(solution)/shard_map/ppermute | solution.py:14
  7.7 18.7 %collective-permute-start.1 = (bf16[2,256,1024]{2,1,0:T(8,128)(2,1)}, bf16[2,256,1024]{2,1,0:T(8,128)(2,1)}, u32[]{:S(2)}, u32[]{:S(2)}) collective-permute-start(bf16[2,256,1024]{2,1,0:T(8,128)(2,1)} %param.4), channel_id=1, source_target_pairs={{2,0},{4,2},{6,4},{8,6},{10,8},{12,10},{14,12},{16,14},{18,16},{20... | collective-permute-start | bytes 3145736 | tf_op jit(solution)/shard_map/ppermute | solution.py:15
  25.5 1.0 copy-start.7
  34.2 7.3 %copy-start = (bf16[40,2,64,1024]{3,2,1,0:T(8,128)(2,1)S(1)}, bf16[40,2,64,1024]{3,2,1,0:T(8,128)(2,1)}, u32[]{:S(2)}) copy-start(bf16[40,2,64,1024]{3,2,1,0:T(8,128)(2,1)} %gather_fusion) | copy-start | bytes 31457284
  34.2 7.5 %copy-start.6 = (bf16[4,64,10,64]{3,2,1,0:T(8,128)(2,1)S(1)}, bf16[4,64,10,64]{3,2,1,0:T(8,128)(2,1)}, u32[]{:S(2)}) copy-start(bf16[4,64,10,64]{3,2,1,0:T(8,128)(2,1)} %reshape.69) | copy-start | bytes 983044
  84.8 2.3 %copy-start.1 = (f32[2,4,64,1024]{3,2,0,1:T(8,128)S(1)}, f32[2,4,64,1024]{3,2,0,1:T(8,128)}, u32[]{:S(2)}) copy-start(f32[2,4,64,1024]{3,2,0,1:T(8,128)} %get-tuple-element.11) | copy-start | bytes 6291460
  87.3 57.5 %copy-start.9 = (f32[2]{0:T(128)}, f32[2]{0:T(128)S(1)}, u32[]{:S(2)}) copy-start(f32[2]{0:T(128)S(1)} %add_divide_fusion) | copy-start | bytes 28
  92.5 4.7 %copy-start.5 = (f32[1,2,256,1024]{3,1,2,0:T(2,128)S(1)}, f32[1,2,256,1024]{3,1,2,0:T(2,128)}, u32[]{:S(2)}) copy-start(f32[1,2,256,1024]{3,1,2,0:T(2,128)} %copy.56) | copy-start | bytes 6291460
  95.9 1.4 copy-start.4
  97.2 9.2 %copy-start.3 = (bf16[4,256,1024]{2,1,0:T(8,128)(2,1)S(1)}, bf16[4,256,1024]{2,1,0:T(8,128)(2,1)}, u32[]{:S(2)}) copy-start(bf16[4,256,1024]{2,1,0:T(8,128)(2,1)} %all-gather.2.cloned.1.call-done) | copy-start | bytes 6291460
  106.4 3.5 %copy-start.2 = (f32[2,4,64,1024]{3,2,1,0:T(8,128)S(1)}, f32[2,4,64,1024]{3,2,1,0:T(8,128)}, u32[]{:S(2)}) copy-start(f32[2,4,64,1024]{3,2,1,0:T(8,128)} %copy.32) | copy-start | bytes 6291460
Sparse Core Ops, SparseCore 0:
  12.9 32.4 all-gather.1
where the time goes:
time: 194 us
  blocking collectives  98.5 us (51%)
  matrix products  31.6 us (16%)
  local copies, waits for them, and re-layouts  28 us (14%)
  between operations  14.2 us (7%)
  waiting for transfers between devices  7.97 us (4%)
  other arithmetic  7.8 us (4%)
  starting transfers between devices  5.57 us (3%)
    psum x3, blocking collectives, row_reduce(): return lax.psum(values, 'space')  98.5 us
    unnamed x25, local copies, waits for them, and re-layouts  16.4 us
    dot_general x1, matrix products, finish(): jnp.dot(wide_all, flat_r.T, precision=lax.Precision.HIGHEST)  9.15 us
    dot_general x1, matrix products, finish(): jnp.dot(coeffs.T, wide_all, precision=lax.Precision.HIGHEST)  8.71 us
    ppermute x1, waiting for transfers between devices, padded(): before = lax.ppermute(last, axis, up)  7.93 us
    dot_general x1, matrix products, apply_tiles(): jnp.einsum('apbq,kabqw->kapw', h_tiles, picked, preferred_element_type=jn...  6.46 us
    gather x1, local copies, waits for them, and re-layouts, apply_tiles(): picked = blocks[:, links]  5.75 us
    ppermute x1, starting transfers between devices, padded(): after = lax.ppermute(first, axis, down)  5.03 us
  transfers between devices with their start and end apart: 3, of which 1 were waited for; matrix products, arithmetic and copies ran while one was open for 15% of the time, Pallas kernels for 0%

commit v1 on v0

--- a/solution.py
+++ b/solution.py
@@ -2,6 +2,12 @@
 import jax.numpy as jnp
 from jax import lax
 from jax.sharding import PartitionSpec as P
+
+
+def summed_here(shard, axis):
+    parts = lax.all_gather(shard, axis, axis=0, tiled=False)
+    total = parts.sum(axis=0)
+    return total
 
 
 def padded(x, sides, width):
@@ -37,7 +43,7 @@
     if section == "ritz":
         return lax.psum(values, "space")
     if section == "project":
-        return lax.psum(values, "space")
+        return summed_here(values, "space")
     return lax.psum(values, "space")
 
 

time: 194 us -> 182 us (0.938)
  blocking collectives: 98.5 us -> 88.3 us
  local copies, waits for them, and re-layouts: 28 us -> 24.2 us
    psum x3 -> x2, blocking collectives: 98.5 us -> 71 us  [row_reduce(): return lax.psum(values, 'space')]
    all_gather x0 -> x1, blocking collectives: none -> 17.4 us  [summed_here(): parts = lax.all_gather(shard, axis, axis=0, tiled=False)]
    unnamed x25 -> x23, local copies, waits for them, and re-layouts: 16.4 us -> 13.6 us
    dot_general x1, matrix products: 3.51 us -> 5.82 us  [finish(): jnp.dot(flat_all, flat_all.T, preferred_element_type=jnp.float32)]
where the time goes in v1:
time: 182 us
  blocking collectives  88.3 us (49%)
  matrix products  32.4 us (18%)
  local copies, waits for them, and re-layouts  24.2 us (13%)
  between operations  14.2 us (8%)
  other arithmetic  9.43 us (5%)
  waiting for transfers between devices  7.95 us (4%)
  starting transfers between devices  5.57 us (3%)
    psum x2, blocking collectives, row_reduce(): return lax.psum(values, 'space')  71 us
    all_gather x1, blocking collectives, summed_here(): parts = lax.all_gather(shard, axis, axis=0, tiled=False)  17.4 us
    unnamed x23, local copies, waits for them, and re-layouts  13.6 us
    dot_general x1, matrix products, finish(): jnp.dot(wide_all, flat_r.T, precision=lax.Precision.HIGHEST)  8.94 us
    dot_general x1, matrix products, finish(): jnp.dot(coeffs.T, wide_all, precision=lax.Precision.HIGHEST)  8.66 us
    ppermute x1, waiting for transfers between devices, padded(): before = lax.ppermute(last, axis, up)  7.93 us
    dot_general x1, matrix products, apply_tiles(): jnp.einsum('apbq,kabqw->kapw', h_tiles, picked, preferred_element_type=jn...  6.45 us
    dot_general x1, matrix products, finish(): jnp.dot(flat_all, flat_all.T, preferred_element_type=jnp.float32)  5.82 us
  transfers between devices with their start and end apart: 3, of which 1 were waited for; matrix products, arithmetic and copies ran while one was open for 15% of the time, Pallas kernels for 0%

profile of v1, /device:TPU:0, one launch (start us, length us, event | category | flops | bytes accessed | tf_op | source)
XLA Modules:
  0.0 182.1 jit_solution(441574596630465263)
XLA Ops:
  7.2 0.0 copy-start.7
  7.2 0.0 all-gather.4.cloned.1.call-start
  7.2 0.5 collective-permute-start
  7.7 5.0 %collective-permute-start.1 = (bf16[2,256,1024]{2,1,0:T(8,128)(2,1)}, bf16[2,256,1024]{2,1,0:T(8,128)(2,1)}, u32[]{:S(2)}, u32[]{:S(2)}) collective-permute-start(bf16[2,256,1024]{2,1,0:T(8,128)(2,1)} %param.4), channel_id=1, source_target_pairs={{2,0},{4,2},{6,4},{8,6},{10,8},{12,10},{14,12},{16,14},{18,16},{20... | collective-permute-start | bytes 3145736 | tf_op jit(solution)/shard_map/ppermute | solution.py:21
  12.8 0.0 all-gather.4.cloned.1.call-update
  12.8 0.7 compare_select_fusion
  13.5 0.1 reshape.56
  13.6 2.4 %reshape.74 = bf16[4,64,10,64]{3,2,1,0:T(8,128)(2,1)} reshape(bf16[256,640]{1,0:T(8,128)(2,1)} %param.5) | data formatting | bytes 655360 | tf_op jit(solution)/shard_map/reshape | solution.py:35
  16.0 0.0 copy-done.7
  16.0 1.6 reshape.73
  17.6 7.9 %collective-permute-done = bf16[2,256,1024]{2,1,0:T(8,128)(2,1)S(1)} collective-permute-done((bf16[2,256,1024]{2,1,0:T(8,128)(2,1)}, bf16[2,256,1024]{2,1,0:T(8,128)(2,1)S(1)}, u32[]{:S(2)}, u32[]{:S(2)}) %collective-permute-start) | collective-permute-done | bytes 1048608 | tf_op jit(solution)/shard_map/ppermute | solution.py:20
  25.5 0.0 copy-start.6
  25.5 1.0 copy-done.6
  26.5 0.0 collective-permute-done.1
  26.5 2.0 %pad_maximum_fusion = bf16[2,768,1024]{2,1,0:T(8,128)(2,1)S(1)} fusion(bf16[2,256,1024]{2,1,0:T(8,128)(2,1)} %collective-permute-done.1, bf16[2,256,1024]{2,1,0:T(8,128)(2,1)} %param.4, bf16[2,256,1024]{2,1,0:T(8,128)(2,1)} %copy-done.6), kind=kLoop, calls=%fused_computation.6 | loop fusion | flops 9437184 | bytes 6291456 | tf_op jit(solution)/shard_map/concatenate | solution.py:22
  28.5 5.8 %gather_fusion = bf16[40,2,64,1024]{3,2,1,0:T(8,128)(2,1)} fusion(bf16[2,12,64,1024]{3,2,1,0:T(8,128)(2,1)S(1)} %bitcast.56, s32[1024]{0:T(1024)S(1)} %pad_clamp_fusion), kind=kCustom, calls=%fused_computation | custom fusion | bytes 20971680 | tf_op jit(solution)/shard_map/gather | solution.py:34
  34.2 0.0 copy-start
  34.2 6.5 %fusion.6 = f32[2,4,64,1024]{3,2,0,1:T(8,128)S(1)} fusion(bf16[2,4,10,64,1024]{4,3,0,2,1:T(8,128)(2,1)} %bitcast.57, bf16[4,64,10,64,1]{3,2,1,0,4:T(8,128)(2,1)} %bitcast.70), kind=kOutput, calls=%fused_computation.14 | convolution fusion | flops 671088640 | bytes 12910592 | tf_op jit(solution)/shard_map/apbq,kabqw->kapw/dot_general | solution.py:37
  40.7 0.0 copy-start.5
  40.7 0.2 copy.32
  40.9 0.6 copy-done
  41.5 0.6 copy-done.5
  42.1 2.3 %multiply_reduce_fusion.1 = (f32[2]{0:T(128)S(1)}, f32[2]{0:T(128)S(1)}, f32[2,4,64,1024]{3,2,0,1:T(8,128)S(1)}) fusion(f32[2,4,64,1024]{3,2,0,1:T(8,128)S(1)} %fusion.6, bf16[2,4,10,64,1024]{4,3,0,2,1:T(8,128)(2,1)S(1)} %bitcast.58, bf16[4,64,10,64,1]{3,2,1,0,4:T(8,128)(2,1)S(1)} %bitcast.69), kind=kOutput, calls=%fused_computation.10 | convolution fusion | flops 673185792 | bytes 15007760 | tf_op jit(solution)/shard_map/apbq,kabqw->kapw/dot_general | solution.py:38
  44.4 0.0 copy-start.1
  44.4 0.2 copy.33
  44.6 1.1 copy-done.1
  45.7 2.9 %copy.55 = f32[1,2,256,1024]{3,1,2,0:T(2,128)} copy(f32[1,2,256,1024]{3,2,1,0:T(8,128)S(1)} %bitcast.61) | data formatting | bytes 4194304
  48.6 3.0 %copy.54 = f32[1,2,256,1024]{3,1,2,0:T(2,128)} copy(f32[1,2,256,1024]{3,2,1,0:T(8,128)S(1)} %bitcast.59) | data formatting | bytes 4194304
  51.6 0.0 all-gather.4.cloned.1.call-done
  51.6 5.8 %fusion.12 = f32[4,4]{0,1:T(4,128)S(1)} fusion(bf16[4,256,1024]{2,1,0:T(8,128)(2,1)} %all-gather.4.cloned.1.call-done), kind=kOutput, calls=%fused_computation.16 | convolution fusion | flops 8388608 | bytes 2097216 | tf_op jit(solution)/shard_map/dot_general | solution.py:57
  57.4 39.6 %all-reduce = (f32[2]{0:T(128)S(1)}, f32[2]{0:T(128)S(1)}, f32[4,4]{0,1:T(4,128)S(1)}) all-reduce(f32[2]{0:T(128)S(1)} %get-tuple-element.4, f32[2]{0:T(128)S(1)} %get-tuple-element.3, f32[4,4]{0,1:T(4,128)S(1)} %fusion.12), channel_id=1, replica_groups=mesh['space'=16,'trial'=2] {'space'}, use_global_device_ids=true, to_apply=%region_1.2 | all-reduce | flops 20 | bytes 160 | tf_op jit(solution)/shard_map/psum | solution.py:44
  97.0 0.1 copy.37
  97.1 0.4 cholesky.16
  97.5 0.6 compare_reduce_fusion
  98.2 0.6 fusion.17
  98.8 0.3 custom-call.10
  99.2 0.0 copy-start.8
  99.2 2.1 %multiply_subtract_fusion = f32[2,4,64,1024]{3,2,0,1:T(8,128)S(1)} fusion(f32[2,4,64,1024]{3,2,0,1:T(8,128)S(1)} %fusion.6, f32[2,4,64,1024]{3,2,0,1:T(8,128)} %copy-done.1, f32[2]{0:T(128)S(1)} %add_divide_fusion), kind=kLoop, calls=%fused_computation.9 | loop fusion | flops 1048576 | bytes 6291464 | tf_op jit(solution)/shard_map/sub | solution.py:63
  101.2 0.1 copy.39
  101.4 0.0 copy-start.2
  101.4 1.6 copy.56
  103.0 0.0 copy-done.2
  103.0 1.6 copy.57
  104.7 0.0 copy-start.4
  104.7 0.0 copy-start.3
  104.7 8.9 %convolution_bitcast_fusion = f32[1,4,2]{1,2,0:T(2,128)S(1)} fusion(f32[2,262144]{1,0:T(2,128)S(1)} %bitcast.68, bf16[4,262144]{1,0:T(4,128)(2,1)S(1)} %bitcast.66), kind=kOutput, calls=%fused_computation.17 | convolution fusion | flops 25165824 | bytes 4194336 | tf_op jit(solution)/shard_map/dot_general | solution.py:64
  113.6 0.0 copy-done.4
  113.6 17.4 %all-gather.1 = f32[16,4,2]{1,2,0:T(2,128)S(1)} all-gather(f32[1,4,2]{1,2,0:T(2,128)S(1)} %convolution_bitcast_fusion), channel_id=2, replica_groups=mesh['space'=16,'trial'=2] {'space'}, dimensions={0}, use_global_device_ids=true | all-gather | bytes 544 | tf_op jit(solution)/shard_map/all_gather | solution.py:8
  131.0 0.1 fusion.19
  131.2 0.1 fusion.21
  131.3 0.0 copy-done.8
  131.3 0.0 copy-done.3
  131.3 8.7 %multiply_reduce_fusion = (f32[2]{0:T(128)S(1)}, f32[2,262144]{1,0:T(2,128)}) fusion(f32[4,2]{0,1:T(2,128)S(1)} %fusion.21, bf16[4,262144]{1,0:T(4,128)(2,1)} %bitcast.67, f32[2,262144]{1,0:T(2,128)} %bitcast.65, f32[2,262144]{1,0:T(2,128)S(1)} %bitcast.64, f32[2]{0:T(128)S(1)} %add_divide_fusion), kind=kOutput, calls=%fused_computation.8 | convolution fusion | flops 27787262 | bytes 8388656 | tf_op jit(solution)/shard_map/dot_general | solution.py:66
  140.0 31.4 %psum.31 = f32[2]{0:T(128)S(1)} all-reduce(f32[2]{0:T(128)S(1)} %get-tuple-element.11), channel_id=1, replica_groups=mesh['space'=16,'trial'=2] {'space'}, use_global_device_ids=true, to_apply=%region_9.10 | all-reduce | flops 2 | bytes 16 | tf_op jit(solution)/shard_map/psum | solution.py:47
  171.4 0.5 add_rsqrt_fusion
  171.9 2.1 %multiply_convert_fusion = bf16[2,262144]{1,0:T(2,128)(2,1)S(1)} fusion(f32[2,262144]{1,0:T(2,128)} %get-tuple-element.12, f32[2]{0:T(128)S(1)} %get-tuple-element.8), kind=kLoop, calls=%fused_computation.7 | loop fusion | flops 1048576 | bytes 3145736 | tf_op jit(solution)/shard_map/convert_element_type | solution.py:69
  174.0 1.2 copy.80
  (5 shorter events, 0.1 us)
Async XLA Ops:
  7.2 8.8 %copy-start.7 = (bf16[256,640]{1,0:T(8,128)(2,1)S(1)}, bf16[256,640]{1,0:T(8,128)(2,1)}, u32[]{:S(2)}) copy-start(bf16[256,640]{1,0:T(8,128)(2,1)} %param.6) | copy-start | bytes 983044
  7.2 44.4 %all-gather.4.cloned.1.call-start = ((), (), s32[]{:S(2)}) async-start(), calls=%async_computation | async-start | bytes 3145728 | tf_op jit(solution)/shard_map/all_gather | solution.py:79
  7.2 18.3 %collective-permute-start = (bf16[2,256,1024]{2,1,0:T(8,128)(2,1)}, bf16[2,256,1024]{2,1,0:T(8,128)(2,1)S(1)}, u32[]{:S(2)}, u32[]{:S(2)}) collective-permute-start(bf16[2,256,1024]{2,1,0:T(8,128)(2,1)} %param.4), channel_id=1, source_target_pairs={{0,2},{2,4},{4,6},{6,8},{8,10},{10,12},{12,14},{14,16},{16,18},{18... | collective-permute-start | bytes 3145736 | tf_op jit(solution)/shard_map/ppermute | solution.py:20
  7.7 18.7 %collective-permute-start.1 = (bf16[2,256,1024]{2,1,0:T(8,128)(2,1)}, bf16[2,256,1024]{2,1,0:T(8,128)(2,1)}, u32[]{:S(2)}, u32[]{:S(2)}) collective-permute-start(bf16[2,256,1024]{2,1,0:T(8,128)(2,1)} %param.4), channel_id=1, source_target_pairs={{2,0},{4,2},{6,4},{8,6},{10,8},{12,10},{14,12},{16,14},{18,16},{20... | collective-permute-start | bytes 3145736 | tf_op jit(solution)/shard_map/ppermute | solution.py:21
  25.5 1.0 copy-start.6
  34.2 7.3 %copy-start = (bf16[40,2,64,1024]{3,2,1,0:T(8,128)(2,1)S(1)}, bf16[40,2,64,1024]{3,2,1,0:T(8,128)(2,1)}, u32[]{:S(2)}) copy-start(bf16[40,2,64,1024]{3,2,1,0:T(8,128)(2,1)} %gather_fusion) | copy-start | bytes 31457284
  40.7 1.4 copy-start.5
  44.4 1.3 copy-start.1
  99.2 32.1 %copy-start.8 = (f32[2]{0:T(128)}, f32[2]{0:T(128)S(1)}, u32[]{:S(2)}) copy-start(f32[2]{0:T(128)S(1)} %add_divide_fusion) | copy-start | bytes 28
  101.4 1.6 copy-start.2
  104.7 9.0 %copy-start.4 = (bf16[1,4,256,1024]{3,1,2,0:T(4,128)(2,1)}, bf16[1,4,256,1024]{3,1,2,0:T(4,128)(2,1)S(1)}, u32[]{:S(2)}) copy-start(bf16[1,4,256,1024]{3,1,2,0:T(4,128)(2,1)S(1)} %copy.57) | copy-start | bytes 6291460
  104.7 26.6 %copy-start.3 = (f32[1,2,256,1024]{3,1,2,0:T(2,128)S(1)}, f32[1,2,256,1024]{3,1,2,0:T(2,128)}, u32[]{:S(2)}) copy-start(f32[1,2,256,1024]{3,1,2,0:T(2,128)} %copy.55) | copy-start | bytes 6291460
Sparse Core Ops, SparseCore 0:
  12.9 32.4 all-gather.3
